TPU v7x, 1024 devices: a whole 4x4x32 slice. The times are simulated.
1024 devices in a mesh: cells: 32 (over y, x, core), region: 32 (over z).
Axes of the slice: x: 4, y: 4, z: 32, core: 2. Of those that a mesh axis runs over, the one named last changes fastest.
Arguments:
- cell_shape: bfloat16 [1024, 3, 544], P(('cells', 'region')), may hold values from -6 to 6
- upsample: bfloat16 [544, 2112], replicated, may hold values from -0.25 to 0.25
- bending: bfloat16 [544, 2112], replicated, may hold values from -0.25 to 0.25
- to_density: bfloat16 [2112, 152], replicated, may hold values from -0.125 to 0.125
- translate: bfloat16 [456, 456], replicated, may hold values from -0.25 to 0.25
- evaluate: bfloat16 [152, 2112], replicated, may hold values from -0.5 to 0.5
- smoothing: bfloat16 [2112, 544], replicated, may hold values from -0.125 to 0.125
- block_owner: int32 [270336, 1], P(('cells', 'region')), may hold values from 0 to 31; in each aligned block of 264 rows (0 to 263, 264 to 527, ...) at most 10 rows name the same one
- block_octant: int32 [270336], P(('cells', 'region')), may hold values from 0 to 63
- far_list: int32 [1024, 8], P(('cells', 'region')), may hold values from 0 to 2047
Outputs:
- velocity: float32 [1024, 3, 544], P(('cells', 'region'))
Inputs may be any that keep to these rules, and one draw needn't show every extreme that they name: `block_owner`: among the 264 blocks of one device no owner is named more than 10 times, and in some device's blocks one owner is named exactly 10 times.
All inputs are finite; a program needn't handle non-finite values.
Results may differ from a plain program's by a relative error of at most 0.0063.
Values may be sent and summed in bfloat16 or wider, within the bound.
A program may use at most 32 MiB of HBM per device.

v0:
```python
from functools import partial

import jax
import jax.numpy as jnp
from jax import lax
from jax.sharding import PartitionSpec as P

P_COARSE = 544
P_FINE = 2112
EQ_PTS = 152
EQUIV = 456
BLK = 8
OCT_DEV = 2


EPSILON_SQ = 0.0625
STOKES_SCALE = 1.0 / (8.0 * 3.141592653589793)


def stokeslet(targets, sources, strength):
    diff_x = targets[0][:, None] - sources[0][None, :]
    diff_y = targets[1][:, None] - sources[1][None, :]
    diff_z = targets[2][:, None] - sources[2][None, :]
    radius_sq = diff_x * diff_x + diff_y * diff_y + diff_z * diff_z + EPSILON_SQ
    inverse = lax.rsqrt(radius_sq)
    cubed = inverse * inverse * inverse
    direct = (radius_sq + EPSILON_SQ) * cubed
    radial = (
        diff_x * strength[0][None, :]
        + diff_y * strength[1][None, :]
        + diff_z * strength[2][None, :]
    ) * cubed
    vel_x = jnp.sum(direct * strength[0][None, :] + diff_x * radial, axis=1)
    vel_y = jnp.sum(direct * strength[1][None, :] + diff_y * radial, axis=1)
    vel_z = jnp.sum(direct * strength[2][None, :] + diff_z * radial, axis=1)
    return jnp.stack([vel_x, vel_y, vel_z]) * STOKES_SCALE


def near_field(leaf_points):
    sources = leaf_points[:3].astype(jnp.float32)
    strength = leaf_points[3:].astype(jnp.float32)
    tile_set = sources.reshape(3, -1, 256).transpose(1, 0, 2)
    result = lax.map(partial(stokeslet, sources=sources, strength=strength), tile_set)
    return result.transpose(1, 0, 2).reshape(3, -1)


def slot_numbers(owner, owners_count, capacity):
    onehot = (owner[:, None] == jnp.arange(owners_count, dtype=jnp.int32)[None, :]).astype(
        jnp.int32
    )
    before = jnp.cumsum(onehot, axis=0) - onehot
    slot_rank = jnp.sum(before * onehot, axis=1)
    return owner * capacity + slot_rank


def same_rows(row_ids):
    return row_ids


def add_listed(portion, listed, id_map):
    row_ids = jnp.arange(portion.shape[0], dtype=jnp.int32)
    octant_id = id_map(row_ids)
    counts = jnp.sum((listed[:, :, None] == octant_id[None, None, :]).astype(jnp.float32), axis=1)
    return jnp.dot(counts.astype(jnp.bfloat16), portion, preferred_element_type=jnp.float32)


def on_device(
    cell_shape,
    upsample,
    bending,
    to_density,
    translate,
    evaluate,
    smoothing,
    block_owner,
    block_octant,
    far_list,
):
    cell_count = cell_shape.shape[0]
    owners_count = lax.axis_size("cells")
    per_cell = P_FINE // BLK
    block_count = block_owner.shape[0]
    capacity = block_count // owners_count + 2
    coarse = cell_shape.reshape(cell_count * 3, P_COARSE)
    points = (
        jnp.dot(coarse, upsample, preferred_element_type=jnp.float32)
        .astype(jnp.bfloat16)
        .reshape(cell_count, 3, P_FINE)
    )
    forces = (
        jnp.dot(coarse, bending, preferred_element_type=jnp.float32)
        .astype(jnp.bfloat16)
        .reshape(cell_count, 3, P_FINE)
    )
    stacked = jnp.concatenate([points, forces], axis=1)
    blocks = (
        stacked.reshape(cell_count, 6, per_cell, BLK)
        .transpose(0, 2, 1, 3)
        .reshape(block_count, 6, BLK)
    )
    slot_index = slot_numbers(block_owner[:, 0], owners_count, capacity)
    outgoing = jnp.zeros((owners_count * capacity, 6, BLK), jnp.bfloat16).at[slot_index].set(blocks)
    outgoing = (
        outgoing.reshape(owners_count, capacity, 6, BLK)
        .transpose(0, 2, 1, 3)
        .reshape(owners_count, 6, capacity * BLK)
    )
    incoming = lax.all_to_all(outgoing, "cells", split_axis=0, concat_axis=0, tiled=True)
    leaf_points = incoming.transpose(1, 0, 2).reshape(6, owners_count * capacity * BLK)
    near_vel = near_field(leaf_points)
    replies = near_vel.reshape(3, owners_count, capacity * BLK).transpose(1, 0, 2)
    returned = lax.all_to_all(replies, "cells", split_axis=0, concat_axis=0, tiled=True)
    returned = (
        returned.reshape(owners_count, 3, capacity, BLK)
        .transpose(0, 2, 1, 3)
        .reshape(owners_count * capacity, 3, BLK)
    )
    own_blocks = returned[slot_index]
    near_points = (
        own_blocks.reshape(cell_count, per_cell, 3, BLK)
        .transpose(0, 2, 1, 3)
        .reshape(cell_count, 3, P_FINE)
    )
    octant_local = OCT_DEV * owners_count
    octant_blocks = block_octant.reshape(cell_count, per_cell, 1)
    point_octant = jnp.broadcast_to(octant_blocks, (cell_count, per_cell, BLK)).reshape(
        cell_count, P_FINE
    )
    choose = point_octant[None] == jnp.arange(octant_local, dtype=jnp.int32)[:, None, None]
    masked = jnp.where(choose[:, :, None, :], forces[None], jnp.zeros((), jnp.bfloat16))
    product = jnp.dot(masked.reshape(-1, P_FINE), to_density, preferred_element_type=jnp.float32)
    density_part = jnp.sum(product.reshape(octant_local, cell_count, EQUIV), axis=1)
    summed = lax.psum(density_part, "cells")
    expansion = jnp.dot(
        summed.astype(jnp.bfloat16), translate, preferred_element_type=jnp.float32
    ).astype(jnp.bfloat16)
    far_sum = add_listed(
        lax.all_gather(expansion, "region", axis=0, tiled=True), listed=far_list, id_map=same_rows
    )
    far_round = far_sum.astype(jnp.bfloat16).reshape(cell_count * 3, EQ_PTS)
    far_velocity = jnp.dot(far_round, evaluate, preferred_element_type=jnp.float32).reshape(
        cell_count, 3, P_FINE
    )
    total = (near_points + far_velocity).astype(jnp.bfloat16)
    velocity = jnp.dot(
        total.reshape(cell_count * 3, P_FINE), smoothing, preferred_element_type=jnp.float32
    )
    return velocity.reshape(cell_count, 3, P_COARSE)


def solution(mesh):
    return jax.shard_map(
        on_device,
        mesh=mesh,
        in_specs=(
            P(("cells", "region"), None, None),
            P(),
            P(),
            P(),
            P(),
            P(),
            P(),
            P(("cells", "region"), None),
            P(("cells", "region")),
            P(("cells", "region"), None),
        ),
        out_specs=P(("cells", "region"), None, None),
        check_vma=False,
    )
```

profile of v0, /device:TPU:8, one launch (start us, length us, event | category | flops | bytes accessed | tf_op | source)
XLA Modules:
  0.0 328.9 jit_solution(1212097111593622318)
XLA Ops:
  6.5 0.8 reduce.7
  7.4 0.9 reduce-window.6
  9.4 1.1 convolution_convert_fusion
  10.9 2.1 convolution_convert_fusion.1
  13.4 1.1 copy.86
  14.6 17.4 %scatter_fusion = bf16[320,6,8]{2,1,0:T(8,128)(2,1)S(1)} fusion(bf16[320,6,8]{2,1,0:T(8,128)(2,1)S(1)} %broadcast_in_dim.41, s32[264]{0:T(512)S(1)} %fusion.24, bf16[264,6,8]{2,1,0:T(8,128)(2,1)} %copy.86), kind=kCustom, calls=%fused_computation.1 | custom fusion | bytes 77088 | tf_op jit(solution)/shard_map/scatter | solution.py:102
  32.6 0.7 reshape.263
  33.3 16.6 %all-to-all-start = ((bf16[32,2,240]{2,1,0:T(2,128)(2,1)}), bf16[32,2,240]{2,1,0:T(2,128)(2,1)S(1)}, u32[]{:S(2)}, u32[]{:S(2)}) async-start(bf16[32,2,240]{2,1,0:T(2,128)(2,1)} %reshape.263), calls=%async_computation | async-start | bytes 65536 | tf_op jit(solution)/shard_map/all_to_all | solution.py:108
  50.3 0.9 broadcast_select_fusion
  51.3 1.5 select_n.17
  52.8 1.7 fusion.25
  54.6 110.8 %psum.7 = bf16[64,456]{1,0:T(8,128)(2,1)S(1)} all-reduce(f32[64,456]{1,0:T(8,128)S(1)} %reduce_sum.65), channel_id=1, replica_groups=mesh['cells'=32,'region'=32] {'cells'}, use_global_device_ids=true, to_apply=%region_10.11 | all-reduce | flops 29184 | bytes 175104 | tf_op jit(solution)/shard_map/psum | solution.py:133
  165.4 1.9 convolution_convert_fusion.2
  167.9 36.2 %while.12 = (s32[]{:T(128)}, f32[10,3,256]{2,1,0:T(4,128)S(1)}, f32[10,3,256]{2,0,1:T(8,128)S(1)}, f32[3,2560]{1,0:T(4,128)S(1)}, f32[3,2560]{1,0:T(4,128)S(1)}, /*index=5*/s32[]{:T(128)}, s32[]{:T(128)}, s32[]{}, s32[]{}) while((s32[]{:T(128)}, f32[10,3,256]{2,1,0:T(4,128)S(1)}, f32[10,3,256]{2,0,1:T(8,128)S(1)}, f32[3,2560]{1,0:T(4,128)S(1)}, ...), condition=%wide.region_8.9_spmd, body=%wide.region_4.8_spmd.sunk | while | flops 20317700 | bytes 203909 | solution.py:43
  168.1 3.4 %fusion.40 = (f32[256]{0:T(256)S(1)}, f32[256]{0:T(256)S(1)}, f32[256]{0:T(256)S(1)}) fusion(f32[2560]{0:T(1024)S(1)} %get-tuple-element.166, f32[2560]{0:T(1024)S(1)} %get-tuple-element.167, f32[256]{0:T(256)S(1)} %bitcast.93, f32[2560]{0:T(1024)S(1)} %get-tuple-element.169, f32[256]{0:T(256)S(1)} %bitcast.94, f32[2560]{0:T(1024)S(1)} %get-tuple-element.171, ...), kind=kLoop, calls=%fused_computation.18.clone.1 | loop fusion | flops 20315392 | bytes 67584 | tf_op jit(solution)/shard_map/while/body/eval_jaxpr/reduce_sum | solution.py:33
  171.7 3.4 %fusion.40 = (f32[256]{0:T(256)S(1)}, f32[256]{0:T(256)S(1)}, f32[256]{0:T(256)S(1)}) fusion(f32[2560]{0:T(1024)S(1)} %get-tuple-element.166, f32[2560]{0:T(1024)S(1)} %get-tuple-element.167, f32[256]{0:T(256)S(1)} %bitcast.93, f32[2560]{0:T(1024)S(1)} %get-tuple-element.169, f32[256]{0:T(256)S(1)} %bitcast.94, f32[2560]{0:T(1024)S(1)} %get-tuple-element.171, ...), kind=kLoop, calls=%fused_computation.18.clone.1 | loop fusion | flops 20315392 | bytes 67584 | tf_op jit(solution)/shard_map/while/body/eval_jaxpr/reduce_sum | solution.py:33
  175.3 3.4 %fusion.40 = (f32[256]{0:T(256)S(1)}, f32[256]{0:T(256)S(1)}, f32[256]{0:T(256)S(1)}) fusion(f32[2560]{0:T(1024)S(1)} %get-tuple-element.166, f32[2560]{0:T(1024)S(1)} %get-tuple-element.167, f32[256]{0:T(256)S(1)} %bitcast.93, f32[2560]{0:T(1024)S(1)} %get-tuple-element.169, f32[256]{0:T(256)S(1)} %bitcast.94, f32[2560]{0:T(1024)S(1)} %get-tuple-element.171, ...), kind=kLoop, calls=%fused_computation.18.clone.1 | loop fusion | flops 20315392 | bytes 67584 | tf_op jit(solution)/shard_map/while/body/eval_jaxpr/reduce_sum | solution.py:33
  179.0 3.4 %fusion.40 = (f32[256]{0:T(256)S(1)}, f32[256]{0:T(256)S(1)}, f32[256]{0:T(256)S(1)}) fusion(f32[2560]{0:T(1024)S(1)} %get-tuple-element.166, f32[2560]{0:T(1024)S(1)} %get-tuple-element.167, f32[256]{0:T(256)S(1)} %bitcast.93, f32[2560]{0:T(1024)S(1)} %get-tuple-element.169, f32[256]{0:T(256)S(1)} %bitcast.94, f32[2560]{0:T(1024)S(1)} %get-tuple-element.171, ...), kind=kLoop, calls=%fused_computation.18.clone.1 | loop fusion | flops 20315392 | bytes 67584 | tf_op jit(solution)/shard_map/while/body/eval_jaxpr/reduce_sum | solution.py:33
  182.6 3.4 %fusion.40 = (f32[256]{0:T(256)S(1)}, f32[256]{0:T(256)S(1)}, f32[256]{0:T(256)S(1)}) fusion(f32[2560]{0:T(1024)S(1)} %get-tuple-element.166, f32[2560]{0:T(1024)S(1)} %get-tuple-element.167, f32[256]{0:T(256)S(1)} %bitcast.93, f32[2560]{0:T(1024)S(1)} %get-tuple-element.169, f32[256]{0:T(256)S(1)} %bitcast.94, f32[2560]{0:T(1024)S(1)} %get-tuple-element.171, ...), kind=kLoop, calls=%fused_computation.18.clone.1 | loop fusion | flops 20315392 | bytes 67584 | tf_op jit(solution)/shard_map/while/body/eval_jaxpr/reduce_sum | solution.py:33
  186.2 3.4 %fusion.40 = (f32[256]{0:T(256)S(1)}, f32[256]{0:T(256)S(1)}, f32[256]{0:T(256)S(1)}) fusion(f32[2560]{0:T(1024)S(1)} %get-tuple-element.166, f32[2560]{0:T(1024)S(1)} %get-tuple-element.167, f32[256]{0:T(256)S(1)} %bitcast.93, f32[2560]{0:T(1024)S(1)} %get-tuple-element.169, f32[256]{0:T(256)S(1)} %bitcast.94, f32[2560]{0:T(1024)S(1)} %get-tuple-element.171, ...), kind=kLoop, calls=%fused_computation.18.clone.1 | loop fusion | flops 20315392 | bytes 67584 | tf_op jit(solution)/shard_map/while/body/eval_jaxpr/reduce_sum | solution.py:33
  189.8 3.4 %fusion.40 = (f32[256]{0:T(256)S(1)}, f32[256]{0:T(256)S(1)}, f32[256]{0:T(256)S(1)}) fusion(f32[2560]{0:T(1024)S(1)} %get-tuple-element.166, f32[2560]{0:T(1024)S(1)} %get-tuple-element.167, f32[256]{0:T(256)S(1)} %bitcast.93, f32[2560]{0:T(1024)S(1)} %get-tuple-element.169, f32[256]{0:T(256)S(1)} %bitcast.94, f32[2560]{0:T(1024)S(1)} %get-tuple-element.171, ...), kind=kLoop, calls=%fused_computation.18.clone.1 | loop fusion | flops 20315392 | bytes 67584 | tf_op jit(solution)/shard_map/while/body/eval_jaxpr/reduce_sum | solution.py:33
  193.4 3.4 %fusion.40 = (f32[256]{0:T(256)S(1)}, f32[256]{0:T(256)S(1)}, f32[256]{0:T(256)S(1)}) fusion(f32[2560]{0:T(1024)S(1)} %get-tuple-element.166, f32[2560]{0:T(1024)S(1)} %get-tuple-element.167, f32[256]{0:T(256)S(1)} %bitcast.93, f32[2560]{0:T(1024)S(1)} %get-tuple-element.169, f32[256]{0:T(256)S(1)} %bitcast.94, f32[2560]{0:T(1024)S(1)} %get-tuple-element.171, ...), kind=kLoop, calls=%fused_computation.18.clone.1 | loop fusion | flops 20315392 | bytes 67584 | tf_op jit(solution)/shard_map/while/body/eval_jaxpr/reduce_sum | solution.py:33
  197.1 3.4 %fusion.40 = (f32[256]{0:T(256)S(1)}, f32[256]{0:T(256)S(1)}, f32[256]{0:T(256)S(1)}) fusion(f32[2560]{0:T(1024)S(1)} %get-tuple-element.166, f32[2560]{0:T(1024)S(1)} %get-tuple-element.167, f32[256]{0:T(256)S(1)} %bitcast.93, f32[2560]{0:T(1024)S(1)} %get-tuple-element.169, f32[256]{0:T(256)S(1)} %bitcast.94, f32[2560]{0:T(1024)S(1)} %get-tuple-element.171, ...), kind=kLoop, calls=%fused_computation.18.clone.1 | loop fusion | flops 20315392 | bytes 67584 | tf_op jit(solution)/shard_map/while/body/eval_jaxpr/reduce_sum | solution.py:33
  200.7 3.4 %fusion.40 = (f32[256]{0:T(256)S(1)}, f32[256]{0:T(256)S(1)}, f32[256]{0:T(256)S(1)}) fusion(f32[2560]{0:T(1024)S(1)} %get-tuple-element.166, f32[2560]{0:T(1024)S(1)} %get-tuple-element.167, f32[256]{0:T(256)S(1)} %bitcast.93, f32[2560]{0:T(1024)S(1)} %get-tuple-element.169, f32[256]{0:T(256)S(1)} %bitcast.94, f32[2560]{0:T(1024)S(1)} %get-tuple-element.171, ...), kind=kLoop, calls=%fused_computation.18.clone.1 | loop fusion | flops 20315392 | bytes 67584 | tf_op jit(solution)/shard_map/while/body/eval_jaxpr/reduce_sum | solution.py:33
  204.3 0.7 reshape.265
  205.0 21.8 %all-to-all-start.1 = ((f32[32,1,240]{2,1,0:T(1,128)}), f32[32,1,240]{2,1,0:T(1,128)S(1)}, u32[]{:S(2)}, u32[]{:S(2)}) async-start(f32[32,1,240]{2,1,0:T(1,128)} %reshape.265), calls=%async_computation.1 | async-start | bytes 65536 | tf_op jit(solution)/shard_map/all_to_all | solution.py:112
  226.8 6.3 %all-to-all-done.1 = f32[32,1,240]{2,1,0:T(1,128)S(1)} async-done(((f32[32,1,240]{2,1,0:T(1,128)}), f32[32,1,240]{2,1,0:T(1,128)S(1)}, u32[]{:S(2)}, u32[]{:S(2)}) %all-to-all-start.1) | async-done | bytes 30752 | tf_op jit(solution)/shard_map/all_to_all | solution.py:112
  234.9 2.4 gather_fusion
  237.3 1.1 copy.97
  238.6 78.2 %all-gather.2.cloned.1.call-done = bf16[2048,456]{1,0:T(8,128)(2,1)} async-done(((bf16[64,456]{1,0:T(8,128)(2,1)}), bf16[2048,456]{1,0:T(8,128)(2,1)}) %all-gather.2.cloned.1.call-update) | async-done | bytes 1867792 | tf_op jit(solution)/shard_map/all_gather | solution.py:138
  316.8 2.0 fusion.26
  318.9 2.6 fusion.18
  (84 shorter events, 8.4 us)
Async XLA Ops:
  6.5 2.9 copy-start
  6.5 4.4 %copy-start.2 = (bf16[1,3,544]{2,1,0:T(4,128)(2,1)S(1)}, bf16[1,3,544]{2,1,0:T(4,128)(2,1)}, u32[]{:S(2)}) copy-start(bf16[1,3,544]{2,1,0:T(4,128)(2,1)} %param.12) | copy-start | bytes 9796
  13.0 37.0 %copy-start.3 = (s32[264]{0:T(512)S(1)}, s32[264]{0:T(512)}, u32[]{:S(2)}) copy-start(s32[264]{0:T(512)} %param.20) | copy-start | bytes 3172
  33.3 134.1 %all-to-all-start = ((bf16[32,2,240]{2,1,0:T(2,128)(2,1)}), bf16[32,2,240]{2,1,0:T(2,128)(2,1)S(1)}, u32[]{:S(2)}, u32[]{:S(2)}) async-start(bf16[32,2,240]{2,1,0:T(2,128)(2,1)} %reshape.263), calls=%async_computation | async-start | bytes 65536 | tf_op jit(solution)/shard_map/all_to_all | solution.py:108
  50.0 266.8 %all-gather.2.cloned.1.call-start = ((), (), s32[]{:S(2)}) async-start(), calls=%async_computation.2 | async-start | bytes 2162688 | tf_op jit(solution)/shard_map/all_gather | solution.py:138
  51.2 116.1 %copy-start.4 = (s32[1,8]{1,0:T(1,128)S(1)}, s32[1,8]{1,0:T(1,128)}, u32[]{:S(2)}) copy-start(s32[1,8]{1,0:T(1,128)} %param.21) | copy-start | bytes 100
  205.0 28.1 %all-to-all-start.1 = ((f32[32,1,240]{2,1,0:T(1,128)}), f32[32,1,240]{2,1,0:T(1,128)S(1)}, u32[]{:S(2)}, u32[]{:S(2)}) async-start(f32[32,1,240]{2,1,0:T(1,128)} %reshape.265), calls=%async_computation.1 | async-start | bytes 65536 | tf_op jit(solution)/shard_map/all_to_all | solution.py:112
  237.3 81.6 %copy-start.1 = (bf16[152,2112]{1,0:T(8,128)(2,1)S(1)}, bf16[152,2112]{1,0:T(8,128)(2,1)}, u32[]{:S(2)}) copy-start(bf16[152,2112]{1,0:T(8,128)(2,1)} %param.17) | copy-start | bytes 1926148
Sparse Core Ops, SparseCore 0:
  167.4 149.3 all-gather.1
where the time goes:
time: 331 us; the launch traced here: 329 us
  blocking collectives  111 us (34%)
  waiting for transfers between devices  84.5 us (26%)
  other arithmetic  38.6 us (12%)
  starting transfers between devices  38.4 us (12%)
  local copies, waits for them, and re-layouts  31.3 us (9%)
  between operations  13.7 us (4%)
  matrix products  11.3 us (3%)
    psum x1, blocking collectives, on_device(): summed = lax.psum(density_part, 'cells')  111 us
    all_gather x1, waiting for transfers between devices, on_device(): lax.all_gather(expansion, 'region', axis=0, tiled=True)  78.2 us
    reduce_sum x10, other arithmetic, stokeslet(): vel_x = jnp.sum(direct * strength[0][None, :] + diff_x * radial, axis=1)  34 us
    all_to_all x1, starting transfers between devices, on_device(): lax.all_to_all(replies, 'cells', split_axis=0, concat_axis=0, tiled=True)  21.8 us
    scatter x1, local copies, waits for them, and re-layouts, on_device(): jnp.zeros((owners_count * capacity, 6, BLK), jnp.bfloat16).at[slot_index]  17.4 us
    all_to_all x1, starting transfers between devices, on_device(): lax.all_to_all(outgoing, 'cells', split_axis=0, concat_axis=0, tiled=True)  16.6 us
  transfers between devices with their start and end apart: 3, of which 2 were waited for; matrix products, arithmetic and copies ran while one was open for 15% of the time, Pallas kernels for 0%

commit v1 on v0

v1 whole, which is shorter than its diff:
```python
import jax
import jax.numpy as jnp
from jax import lax
from jax.experimental import pallas as pl
from jax.experimental.pallas import tpu as pltpu
from jax.sharding import PartitionSpec as P

P_COARSE = 544
P_FINE = 2112
EQ_PTS = 152
EQUIV = 456
NB = 264
NC = 32
NR = 32
SLOT = 16
CAP = 10
LEAF = NC * CAP * 8
NEAR = 4
TILE = 256
EPSILON_SQ = 0.0625
STOKES_SCALE = 1.0 / (8.0 * 3.141592653589793)

MESH = pl.DeviceIdType.MESH
F32 = jnp.float32
BF = jnp.bfloat16
I32 = jnp.int32


def iota(shape, axis):
    return lax.broadcasted_iota(I32, shape, axis)


def onehot(mask):
    return jnp.where(mask, 1.0, 0.0).astype(BF)


def dot(a, b):
    return jnp.dot(a, b, preferred_element_type=F32)


def dot_nt(a, b):
    return lax.dot_general(a, b, (((1,), (1,)), ((), ())), preferred_element_type=F32)


def pieces(value, count):
    found = []
    for at in range(count):
        part = value.astype(BF).astype(F32)
        found.append(part)
        if at + 1 < count:
            value = value - part
    return found


def spread_points(rows, lanes):
    keep = (iota((8, lanes), 1) & 7) == iota((8, lanes), 0)
    made = [jnp.where(keep, jnp.broadcast_to(row, (8, lanes)), 0.0) for row in rows]
    return jnp.concatenate(made, axis=0)


def gather_points(spread, lanes):
    keep = (iota((8, lanes), 1) & 7) == iota((8, lanes), 0)
    return [
        jnp.sum(jnp.where(keep, spread[8 * a : 8 * a + 8, :], 0.0), axis=0, keepdims=True)
        for a in range(spread.shape[0] // 8)
    ]


def kernel(
    cell_ref, owner_row_ref, owner_col_ref, octant_ref, far_ref,
    up_hbm, bend_hbm, td_hbm, tr_hbm, ev_hbm, sm_hbm,
    out_ref,
    up, bend, td, tr, ev, sm,
    expand, expand_leaf, place, masked,
    msg_d, msg_b, msg_r, msg_f, got_d, got_b, got_r, got_f, held,
    left_rows, right_rows, right_cols, weight_rows, weights, moments,
    counts, far_map, smooth_hi, smooth_lo,
    load_sem, sd, rd, sb, rb, sr, rr, sf, rf, sz, rz,
):
    me = lax.axis_index("cells")
    zr = lax.axis_index("region")

    def plus(k):
        return lax.rem(me + k, NC)

    def minus(k):
        return lax.rem(me + NC - k, NC)

    barrier = pltpu.get_barrier_semaphore()

    def greet(k, _):
        pl.semaphore_signal(barrier, inc=1, device_id=(plus(k), zr), device_id_type=MESH)
        return 0

    lax.fori_loop(1, NC, greet, 0)
    for d in range(1, NEAR + 1):
        for there in (lax.rem(zr + d, NR), lax.rem(zr + NR - d, NR)):
            pl.semaphore_signal(barrier, inc=1, device_id=(me, there), device_id_type=MESH)

    loads = [
        pltpu.make_async_copy(src, dst, load_sem.at[at])
        for at, (src, dst) in enumerate(
            ((bend_hbm, bend), (td_hbm, td), (up_hbm, up), (tr_hbm, tr), (ev_hbm, ev), (sm_hbm, sm))
        )
    ]
    for load in loads:
        load.start()

    def plane_copy(src, dst, send, recv, k, target):
        return pltpu.make_async_remote_copy(
            src_ref=src.at[k], dst_ref=dst.at[k], send_sem=send.at[k], recv_sem=recv.at[k],
            device_id=(target, zr), device_id_type=MESH,
        )

    def send_all(src, dst, send, recv, target_of):
        def step(k, _):
            plane_copy(src, dst, send, recv, k, target_of(k)).start()
            return 0

        lax.fori_loop(1, NC, step, 0)

    def recv_all(src, dst, send, recv, target_of):
        def step(k, _):
            plane_copy(src, dst, send, recv, k, target_of(k)).wait_recv()
            return 0

        lax.fori_loop(1, NC, step, 0)

    def sent_all(src, dst, send, recv, target_of):
        def step(k, _):
            plane_copy(src, dst, send, recv, k, target_of(k)).wait_send()
            return 0

        lax.fori_loop(1, NC, step, 0)

    expand[...] = onehot((iota((NB, P_FINE), 1) >> 3) == iota((NB, P_FINE), 0))
    octants = jnp.broadcast_to(octant_ref[...].astype(F32), (8, NB)).astype(BF)
    point_octant = dot(octants, expand[...])[0:1, :] - (2 * me).astype(F32)
    point_octant = jnp.where(point_octant < 0.0, point_octant + 2.0 * NC, point_octant)

    loads[0].wait()
    coarse = cell_ref[0]
    forces = dot(coarse, bend[...]).astype(BF).astype(F32)
    zero_row = jnp.zeros((1, P_FINE), F32)
    by_row = [forces[a // 2 : a // 2 + 1, :] for a in range(6)] + [zero_row, zero_row]
    by_row = jnp.concatenate(by_row + by_row, axis=0)
    sub = iota((16, P_FINE), 0)
    relative = jnp.broadcast_to(point_octant, (16, P_FINE)) - (2 * (sub >> 3) + (sub & 1)).astype(F32)
    for pair in range(NC // 2):
        masked[16 * pair : 16 * pair + 16, :] = jnp.where(relative == 4.0 * pair, by_row, 0.0).astype(BF)
    loads[1].wait()
    part = dot(masked[...], td[...])
    head = part[:, :128]
    tail = jnp.concatenate([part[:, 128:EQ_PTS], jnp.zeros((8 * NC, 256 - EQ_PTS), F32)], axis=1)
    row = iota((8 * NC, 128), 0) & 7
    lane = iota((8 * NC, 128), 1)
    joined = jnp.where(row < 6, head, 0.0)
    for comp in range(3):
        moved = pltpu.roll(tail, 6 - 2 * comp, axis=0)
        if comp:
            moved = pltpu.roll(moved, 24 * comp, axis=1)
        here = (row >= 6) & (lane >= 24 * comp) & (lane < 24 * comp + 24)
        joined = jnp.where(here, moved, joined)
    msg_d[...] = joined.reshape(NC, 8, 128).astype(BF)

    pl.semaphore_wait(barrier, NC - 1 + 2 * NEAR)
    send_all(msg_d, got_d, sd, rd, plus)
    got_d[0] = msg_d[0]

    owner = lax.rem(owner_row_ref[...] + (NC - me), NC)
    owner_col = lax.rem(owner_col_ref[...] + (NC - me), NC)
    same = (owner_col == owner) & (iota((NB, NB), 0) < iota((NB, NB), 1))
    rank = jnp.sum(jnp.where(same, 1.0, 0.0), axis=0, keepdims=True).astype(I32)
    slot = owner * SLOT + rank
    place[...] = onehot(iota((NC * SLOT, NB), 0) == slot)
    loads[2].wait()
    points = dot(coarse, up[...]).astype(BF).astype(F32)
    rows = [points[a : a + 1, :] for a in range(3)] + [forces[a : a + 1, :] for a in range(3)]
    by_block = dot_nt(spread_points(rows, P_FINE).astype(BF), expand[...])
    by_block = jnp.concatenate([by_block, jnp.zeros((80, NB), F32)], axis=0).astype(BF)
    listed = far_ref[...]
    lane = iota((1, 128), 1)
    far_row = jnp.zeros((1, 128), F32)
    for entry in range(8):
        number = listed[0:1, entry : entry + 1]
        far_row = jnp.where(lane == 64 + entry, (number >> 6).astype(F32), far_row)
        far_row = jnp.where(lane == 72 + entry, (number & 63).astype(F32), far_row)
    routed = dot_nt(place[...], by_block) + far_row
    msg_b[...] = routed.reshape(NC, SLOT, 128).astype(BF)
    send_all(msg_b, got_b, sb, rb, plus)
    got_b[0] = msg_b[0]

    for at in range(NC * SLOT // 64):
        place_row = iota((64, LEAF), 0) + 64 * at
        rank_of = place_row & (SLOT - 1)
        first = jnp.where(rank_of < CAP, (place_row >> 4) * CAP + rank_of, -1)
        expand_leaf[64 * at : 64 * at + 64, :] = onehot((iota((64, LEAF), 1) >> 3) == first)

    recv_all(msg_d, got_d, sd, rd, plus)
    held[0] = jnp.sum(got_d[...].astype(F32), axis=0).astype(BF)

    def z_copy(src, dst, count, at, there):
        return pltpu.make_async_remote_copy(
            src_ref=held.at[pl.ds(src, count)], dst_ref=held.at[pl.ds(dst, count)],
            send_sem=sz.at[at], recv_sem=rz.at[at], device_id=(me, there), device_id_type=MESH,
        )

    ahead, behind = lax.rem(zr + NEAR, NR), lax.rem(zr + NR - NEAR, NR)
    stages = [[]]
    for d in range(1, NEAR + 1):
        stages[0].append(z_copy(0, NR - d, 1, 2 * d - 2, lax.rem(zr + d, NR)))
        stages[0].append(z_copy(0, d, 1, 2 * d - 1, lax.rem(zr + NR - d, NR)))
    for s in range(1, 4):
        count = 4 if s < 3 else 3
        at = 2 * NEAR + 2 * (s - 1)
        stages.append(
            [z_copy(32 - 4 * s, 28 - 4 * s, 4, at, ahead), z_copy(4 * s - 3, 4 * s + 1, count, at + 1, behind)]
        )

    def z_start(s):
        for copy in stages[s]:
            copy.start()

    def z_next(s):
        for copy in stages[s]:
            copy.wait_recv()
        if s < 3:
            z_start(s + 1)

    z_start(0)

    recv_all(msg_b, got_b, sb, rb, plus)
    arrived = got_b[...].reshape(NC * SLOT, 128)
    unit = onehot(iota((128, 128), 0) == iota((128, 128), 1))
    arrived_rows = dot_nt(unit, arrived)[:48, :].astype(BF)
    x0, x1, x2, f0, f1, f2 = gather_points(dot(arrived_rows, expand_leaf[...]), LEAF)
    x, f = (x0, x1, x2), (f0, f1, f2)
    size = x0 * x0 + x1 * x1 + x2 * x2
    work = x0 * f0 + x1 * f1 + x2 * f2
    one = jnp.ones((1, LEAF), F32)
    left = list(x) + pieces(size + EPSILON_SQ, 3) + [one, one, one]
    right = [-2.0 * v for v in x] + [one, one, one] + pieces(size, 3)
    left_rows[...] = jnp.concatenate(left + [jnp.zeros((7, LEAF), F32)], axis=0).astype(BF)
    right_rows[0:16, :] = jnp.concatenate(right + [jnp.zeros((7, LEAF), F32)], axis=0)
    features = list(f) + pieces(work, 3)
    for a in range(3):
        for b in range(3):
            features += pieces(x[a] * f[b], 2)
    for b in range(3):
        features += pieces(size * f[b] + x[b] * work, 3)
    for at, feature in enumerate(features):
        weight_rows[at : at + 1, :] = feature
    weight_rows[33:48, :] = jnp.zeros((15, LEAF), F32)
    weights[...] = weight_rows[...].astype(BF)
    for at in range(LEAF // TILE):
        span = slice(TILE * at, TILE * at + TILE)
        right_cols[span, :] = jnp.transpose(right_rows[:, span]).astype(BF)

    def near_tile(at, _):
        span = pl.ds(pl.multiple_of(at * TILE, TILE), TILE)
        target = left_rows[:, span]
        total = jnp.zeros((48, TILE), F32)
        for source in range(LEAF // TILE):
            piece = slice(TILE * source, TILE * source + TILE)
            spread = jnp.maximum(dot(right_cols[piece, 0:16], target), EPSILON_SQ)
            inverse = lax.rsqrt(spread)
            cubed = (inverse * inverse * inverse).astype(BF)
            total = total + dot(weights[:, piece], cubed)
        moments[:, span] = total
        return 0

    lax.fori_loop(0, 4, near_tile, 0)
    z_next(0)
    lax.fori_loop(4, 10, near_tile, 0)
    z_next(1)

    def moment(at, count=1):
        total = moments[at : at + 1, :]
        for more in range(1, count):
            total = total + moments[at + more : at + more + 1, :]
        return total

    plain = [moment(b) for b in range(3)]
    work_sum = moment(3, 3)
    cross = [[moment(6 + 2 * (3 * a + b), 2) for b in range(3)] for a in range(3)]
    high = [moment(24 + 3 * b, 3) for b in range(3)]
    along = x0 * plain[0] + x1 * plain[1] + x2 * plain[2] - work_sum
    near_hi, near_lo = [], []
    for b in range(3):
        value = (size + 2.0 * EPSILON_SQ) * plain[b] + high[b] + x[b] * along
        for a in range(3):
            value = value - x[a] * (2.0 * cross[a][b] + cross[b][a])
        hi, lo = pieces(value * STOKES_SCALE, 2)
        near_hi.append(hi)
        near_lo.append(lo)
    replies = spread_points(near_hi + near_lo, LEAF)
    replies = jnp.concatenate([replies, jnp.zeros((80, LEAF), F32)], axis=0).astype(BF)
    msg_r[...] = dot_nt(expand_leaf[...], replies).reshape(NC, SLOT, 128).astype(BF)
    send_all(msg_r, got_r, sr, rr, minus)
    got_r[0] = msg_r[0]

    for load in loads[3:]:
        load.wait()
    spot, width = iota((512, EQUIV), 0), iota((512, EQUIV), 1)
    group, inner = spot >> 7, spot & 127
    third = jnp.where(inner < 24, 0, jnp.where(inner < 48, 1, 2))
    flat = jnp.where(group < 3, group * EQ_PTS + inner, third * EQ_PTS + 128 + inner - 24 * third)
    flat = jnp.where((group == 3) & (inner >= 72), -1, flat)
    ordered = dot(onehot(flat == width), tr[...]).astype(BF)
    entry, column = iota((EQUIV, 768), 0), iota((EQUIV, 768), 1)
    wanted = (column >> 8) * EQ_PTS + (column & 255)
    far_map[...] = dot(ordered, onehot((entry == wanted) & ((column & 255) < EQ_PTS))).astype(BF)
    smooth = dot(ev[...], sm[...])
    smooth_hi[0:EQ_PTS, :] = smooth.astype(BF)
    smooth_lo[0:EQ_PTS, :] = (smooth - smooth.astype(BF).astype(F32)).astype(BF)
    z_next(2)

    keys = got_b[...].astype(F32)[:, 0:8, :].reshape(8 * NC, 128)
    column = iota((1, 8 * NR), 1)
    held_key = (lax.rem((column >> 3) + zr, NR) * 64 + 2 * me + (column & 1)).astype(F32)
    total = jnp.zeros((8 * NC, 8 * NR), F32)
    for entry in range(8):
        key = keys[:, 64 + entry : 65 + entry] * 64.0 + keys[:, 72 + entry : 73 + entry]
        total = total + jnp.where(key == held_key, 1.0, 0.0)
    shape = (8 * NC, 8 * NR)
    fits = ((iota(shape, 1) & 7) >> 1) == (iota(shape, 0) & 7)
    counts[...] = jnp.where(fits, total, 0.0).astype(BF)

    recv_all(msg_r, got_r, sr, rr, minus)
    returned = got_r[...].reshape(NC * SLOT, 128)
    returned_rows = dot_nt(unit, returned)[:48, :].astype(BF)
    own = dot(returned_rows, place[...]).astype(BF)
    near = gather_points(dot(own, expand[...]), P_FINE)
    near = [near[b] + near[3 + b] for b in range(3)]
    near = jnp.concatenate(near + [jnp.zeros((5, P_FINE), F32)], axis=0).astype(BF)
    velocity = dot(near, sm[...])

    z_next(3)
    octant_rows = held[...].astype(F32).reshape(8 * NR, 128).astype(BF)
    msg_f[...] = dot(counts[...], octant_rows).reshape(NC, 8, 128).astype(BF)
    send_all(msg_f, got_f, sf, rf, minus)
    got_f[0] = msg_f[0]
    recv_all(msg_f, got_f, sf, rf, minus)
    summed = jnp.sum(got_f[...].astype(F32), axis=0)
    turn = iota((8, 128), 0)
    line = jnp.concatenate([jnp.where(turn == g, summed, 0.0) for g in range(4)], axis=1)
    hi, lo = pieces(line, 2)
    moved = dot(jnp.concatenate([hi, lo], axis=0).astype(BF), far_map[...])
    moved = jnp.sum(moved, axis=0, keepdims=True)
    far = [moved[:, 256 * b : 256 * b + EQ_PTS] for b in range(3)]
    far = jnp.concatenate(far + [jnp.zeros((5, EQ_PTS), F32)], axis=0).astype(BF)
    velocity = velocity + dot(far, smooth_hi[...]) + dot(far, smooth_lo[...])
    out_ref[0] = velocity[0:3, :]

    sent_all(msg_d, got_d, sd, rd, plus)
    sent_all(msg_b, got_b, sb, rb, plus)
    sent_all(msg_r, got_r, sr, rr, minus)
    sent_all(msg_f, got_f, sf, rf, minus)
    for stage in stages:
        for copy in stage:
            copy.wait_send()


def on_device(
    cell_shape, upsample, bending, to_density, translate, evaluate, smoothing,
    block_owner, block_octant, far_list,
):
    vmem = pl.BlockSpec(memory_space=pltpu.VMEM)
    anywhere = pl.BlockSpec(memory_space=pl.ANY)
    owner_row = block_owner.reshape(1, NB)
    octant = block_octant.reshape(1, NB)
    dma = pltpu.SemaphoreType.DMA
    return pl.pallas_call(
        kernel,
        out_shape=jax.ShapeDtypeStruct((1, 3, P_COARSE), F32),
        in_specs=[vmem] * 5 + [anywhere] * 6,
        out_specs=vmem,
        scratch_shapes=[
            pltpu.VMEM((P_COARSE, P_FINE), BF),
            pltpu.VMEM((P_COARSE, P_FINE), BF),
            pltpu.VMEM((P_FINE, EQ_PTS), BF),
            pltpu.VMEM((EQUIV, EQUIV), BF),
            pltpu.VMEM((EQ_PTS, P_FINE), BF),
            pltpu.VMEM((P_FINE, P_COARSE), BF),
            pltpu.VMEM((NB, P_FINE), BF),
            pltpu.VMEM((NC * SLOT, LEAF), BF),
            pltpu.VMEM((NC * SLOT, NB), BF),
            pltpu.VMEM((8 * NC, P_FINE), BF),
            pltpu.VMEM((NC, 8, 128), BF),
            pltpu.VMEM((NC, SLOT, 128), BF),
            pltpu.VMEM((NC, SLOT, 128), BF),
            pltpu.VMEM((NC, 8, 128), BF),
            pltpu.VMEM((NC, 8, 128), BF),
            pltpu.VMEM((NC, SLOT, 128), BF),
            pltpu.VMEM((NC, SLOT, 128), BF),
            pltpu.VMEM((NC, 8, 128), BF),
            pltpu.VMEM((NR, 8, 128), BF),
            pltpu.VMEM((16, LEAF), BF),
            pltpu.VMEM((128, LEAF), F32),
            pltpu.VMEM((LEAF, 128), BF),
            pltpu.VMEM((48, LEAF), F32),
            pltpu.VMEM((48, LEAF), BF),
            pltpu.VMEM((48, LEAF), F32),
            pltpu.VMEM((8 * NC, 8 * NR), BF),
            pltpu.VMEM((512, 768), BF),
            pltpu.VMEM((EQ_PTS, P_COARSE), BF),
            pltpu.VMEM((EQ_PTS, P_COARSE), BF),
            dma((6,)),
        ]
        + [dma((NC,))] * 8
        + [dma((14,))] * 2,
        compiler_params=pltpu.CompilerParams(
            collective_id=0, has_side_effects=True, vmem_limit_bytes=60 * 1024 * 1024
        ),
    )(cell_shape, owner_row, block_owner, octant, far_list,
      upsample, bending, to_density, translate, evaluate, smoothing)


def solution(mesh):
    split = ("cells", "region")
    return jax.shard_map(
        on_device,
        mesh=mesh,
        in_specs=(
            P(split, None, None), P(), P(), P(), P(), P(), P(),
            P(split, None), P(split), P(split, None),
        ),
        out_specs=P(split, None, None),
        check_vma=False,
    )
```

time: 331 us -> 72.6 us (0.22)
  the two profiles are of different devices: /device:TPU:8 before, /device:TPU:1 now
where the time goes in v1:
time: 72.6 us; the launch traced here: 72.3 us
  Pallas kernels  61.6 us (85%)
  local copies, waits for them, and re-layouts  10.7 us (15%)
    pallas_call x1, Pallas kernels, on_device(): pl.pallas_call(kernel, out_shape=jax.ShapeDtypeStruct((1, 3, P_COARSE), F...  61.6 us
    unnamed x3, local copies, waits for them, and re-layouts  8.1 us

profile of v1, /device:TPU:1, one launch (start us, length us, event | category | flops | bytes accessed | tf_op | source)
XLA Modules:
  0.0 72.3 jit_solution(2747162584616201601)
XLA Ops:
  0.0 1.2 %reshape.7.octant_ref = s32[1,264]{1,0:T(1,128)} reshape(s32[264]{0:T(512)} %param.18) | data formatting | bytes 2112 | tf_op jit(solution)/shard_map/reshape | solution.py:371
  1.2 1.5 %copy.11.owner_col_ref = s32[264,1]{1,0:T(8,128)} copy(s32[264,1]{0,1:T(1,128)} %param.17) | data formatting | bytes 2112 | tf_op args[7]
  2.7 2.3 %copy.12.td_hbm = bf16[2112,152]{1,0:T(8,128)(2,1)} copy(bf16[2112,152]{0,1:T(8,128)(2,1)} %param.13) | data formatting | bytes 1284096 | tf_op args[3]
  5.0 4.4 %copy.13.sm_hbm = bf16[2112,544]{1,0:T(8,128)(2,1)} copy(bf16[2112,544]{0,1:T(8,128)(2,1)} %param.16) | data formatting | bytes 4595712 | tf_op args[6]
  9.3 61.6 %shard_map.100 = f32[1,3,544]{2,1,0:T(4,128)} custom-call(bf16[1,3,544]{2,1,0:T(4,128)(2,1)} %cell_ref.1, s32[1,264]{1,0:T(1,128)} %bitcast.1, s32[264,1]{1,0:T(8,128)} %copy.11.owner_col_ref, s32[1,264]{1,0:T(1,128)} %reshape.7.octant_ref, s32[1,8]{1,0:T(1,128)} %far_ref.1, bf16[544,2112]{1,0:T(8,128)(2,1)} %up_hbm.1, bf16[544,2112]{1,0:T(8,128)(2,1)} %bend_hbm.1, ...), custom_call_target="tpu_custom_call" | custom-call | tf_op jit(solution)/shard_map/pallas_call | solution.py:373
  71.0 1.3 %copy.14 = f32[1,3,544]{2,0,1:T(1,128)} copy(f32[1,3,544]{2,1,0:T(4,128)} %shard_map.100) | data formatting | bytes 13056 | tf_op jit(solution)/shard_map/pallas_call | solution.py:373

commit v2 on v1

--- a/solution.py
+++ b/solution.py
@@ -67,7 +67,7 @@
 
 
 def kernel(
-    cell_ref, owner_row_ref, owner_col_ref, octant_ref, far_ref,
+    cell_ref, owner_ref, octant_ref, far_ref,
     up_hbm, bend_hbm, td_hbm, tr_hbm, ev_hbm, sm_hbm,
     out_ref,
     up, bend, td, tr, ev, sm,
@@ -86,25 +86,25 @@
     def minus(k):
         return lax.rem(me + NC - k, NC)
 
-    barrier = pltpu.get_barrier_semaphore()
-
-    def greet(k, _):
-        pl.semaphore_signal(barrier, inc=1, device_id=(plus(k), zr), device_id_type=MESH)
-        return 0
-
-    lax.fori_loop(1, NC, greet, 0)
-    for d in range(1, NEAR + 1):
-        for there in (lax.rem(zr + d, NR), lax.rem(zr + NR - d, NR)):
-            pl.semaphore_signal(barrier, inc=1, device_id=(me, there), device_id_type=MESH)
-
     loads = [
         pltpu.make_async_copy(src, dst, load_sem.at[at])
         for at, (src, dst) in enumerate(
             ((bend_hbm, bend), (td_hbm, td), (up_hbm, up), (tr_hbm, tr), (ev_hbm, ev), (sm_hbm, sm))
         )
     ]
-    for load in loads:
-        load.start()
+    loads[0].start()
+    loads[1].start()
+
+    barrier = pltpu.get_barrier_semaphore()
+
+    def greet(k, _):
+        pl.semaphore_signal(barrier, inc=1, device_id=(plus(k), zr), device_id_type=MESH)
+        return 0
+
+    lax.fori_loop(1, NC, greet, 0)
+    for d in range(1, NEAR + 1):
+        for there in (lax.rem(zr + d, NR), lax.rem(zr + NR - d, NR)):
+            pl.semaphore_signal(barrier, inc=1, device_id=(me, there), device_id_type=MESH)
 
     def plane_copy(src, dst, send, recv, k, target):
         return pltpu.make_async_remote_copy(
@@ -134,11 +134,12 @@
         lax.fori_loop(1, NC, step, 0)
 
     expand[...] = onehot((iota((NB, P_FINE), 1) >> 3) == iota((NB, P_FINE), 0))
-    octants = jnp.broadcast_to(octant_ref[...].astype(F32), (8, NB)).astype(BF)
+    octants = jnp.broadcast_to(octant_ref[...].reshape(1, NB).astype(F32), (8, NB)).astype(BF)
     point_octant = dot(octants, expand[...])[0:1, :] - (2 * me).astype(F32)
     point_octant = jnp.where(point_octant < 0.0, point_octant + 2.0 * NC, point_octant)
 
     loads[0].wait()
+    loads[2].start()
     coarse = cell_ref[0]
     forces = dot(coarse, bend[...]).astype(BF).astype(F32)
     zero_row = jnp.zeros((1, P_FINE), F32)
@@ -149,7 +150,7 @@
     for pair in range(NC // 2):
         masked[16 * pair : 16 * pair + 16, :] = jnp.where(relative == 4.0 * pair, by_row, 0.0).astype(BF)
     loads[1].wait()
-    part = dot(masked[...], td[...])
+    part = dot_nt(masked[...], td[...])
     head = part[:, :128]
     tail = jnp.concatenate([part[:, 128:EQ_PTS], jnp.zeros((8 * NC, 256 - EQ_PTS), F32)], axis=1)
     row = iota((8 * NC, 128), 0) & 7
@@ -167,13 +168,15 @@
     send_all(msg_d, got_d, sd, rd, plus)
     got_d[0] = msg_d[0]
 
-    owner = lax.rem(owner_row_ref[...] + (NC - me), NC)
-    owner_col = lax.rem(owner_col_ref[...] + (NC - me), NC)
-    same = (owner_col == owner) & (iota((NB, NB), 0) < iota((NB, NB), 1))
-    rank = jnp.sum(jnp.where(same, 1.0, 0.0), axis=0, keepdims=True).astype(I32)
+    owner = lax.rem(owner_ref[...] + (NC - me), NC)
+    mine = jnp.where(iota((NC, NB), 0) == owner, 1.0, 0.0)
+    ahead_of = dot(mine.astype(BF), onehot(iota((NB, NB), 0) < iota((NB, NB), 1)))
+    rank = jnp.sum(mine * ahead_of, axis=0, keepdims=True).astype(I32)
     slot = owner * SLOT + rank
     place[...] = onehot(iota((NC * SLOT, NB), 0) == slot)
     loads[2].wait()
+    for load in loads[3:]:
+        load.start()
     points = dot(coarse, up[...]).astype(BF).astype(F32)
     rows = [points[a : a + 1, :] for a in range(3)] + [forces[a : a + 1, :] for a in range(3)]
     by_block = dot_nt(spread_points(rows, P_FINE).astype(BF), expand[...])
@@ -269,10 +272,12 @@
         moments[:, span] = total
         return 0
 
-    lax.fori_loop(0, 4, near_tile, 0)
-    z_next(0)
-    lax.fori_loop(4, 10, near_tile, 0)
-    z_next(1)
+    done = 0
+    for stage, upto in enumerate((1, 5, 9)):
+        lax.fori_loop(done, upto, near_tile, 0)
+        z_next(stage)
+        done = upto
+    lax.fori_loop(done, LEAF // TILE, near_tile, 0)
 
     def moment(at, count=1):
         total = moments[at : at + 1, :]
@@ -299,6 +304,17 @@
     send_all(msg_r, got_r, sr, rr, minus)
     got_r[0] = msg_r[0]
 
+    keys = got_b[...].astype(F32)[:, 0:8, :].reshape(8 * NC, 128)
+    column = iota((1, 8 * NR), 1)
+    held_key = (lax.rem((column >> 3) + zr, NR) * 64 + 2 * me + (column & 1)).astype(F32)
+    total = jnp.zeros((8 * NC, 8 * NR), F32)
+    for entry in range(8):
+        key = keys[:, 64 + entry : 65 + entry] * 64.0 + keys[:, 72 + entry : 73 + entry]
+        total = total + jnp.where(key == held_key, 1.0, 0.0)
+    shape = (8 * NC, 8 * NR)
+    fits = ((iota(shape, 1) & 7) >> 1) == (iota(shape, 0) & 7)
+    counts[...] = jnp.where(fits, total, 0.0).astype(BF)
+
     for load in loads[3:]:
         load.wait()
     spot, width = iota((512, EQUIV), 0), iota((512, EQUIV), 1)
@@ -310,21 +326,21 @@
     entry, column = iota((EQUIV, 768), 0), iota((EQUIV, 768), 1)
     wanted = (column >> 8) * EQ_PTS + (column & 255)
     far_map[...] = dot(ordered, onehot((entry == wanted) & ((column & 255) < EQ_PTS))).astype(BF)
-    smooth = dot(ev[...], sm[...])
+    smooth = dot_nt(ev[...], sm[...])
     smooth_hi[0:EQ_PTS, :] = smooth.astype(BF)
     smooth_lo[0:EQ_PTS, :] = (smooth - smooth.astype(BF).astype(F32)).astype(BF)
-    z_next(2)
-
-    keys = got_b[...].astype(F32)[:, 0:8, :].reshape(8 * NC, 128)
-    column = iota((1, 8 * NR), 1)
-    held_key = (lax.rem((column >> 3) + zr, NR) * 64 + 2 * me + (column & 1)).astype(F32)
-    total = jnp.zeros((8 * NC, 8 * NR), F32)
-    for entry in range(8):
-        key = keys[:, 64 + entry : 65 + entry] * 64.0 + keys[:, 72 + entry : 73 + entry]
-        total = total + jnp.where(key == held_key, 1.0, 0.0)
-    shape = (8 * NC, 8 * NR)
-    fits = ((iota(shape, 1) & 7) >> 1) == (iota(shape, 0) & 7)
-    counts[...] = jnp.where(fits, total, 0.0).astype(BF)
+    z_next(3)
+    octant_rows = held[...].astype(F32).reshape(8 * NR, 128).astype(BF)
+    msg_f[...] = dot(counts[...], octant_rows).reshape(NC, 8, 128).astype(BF)
+    send_all(msg_f, got_f, sf, rf, minus)
+    got_f[0] = msg_f[0]
+
+    sent_all(msg_d, got_d, sd, rd, plus)
+    sent_all(msg_b, got_b, sb, rb, plus)
+    sent_all(msg_r, got_r, sr, rr, minus)
+    for stage in stages:
+        for copy in stage:
+            copy.wait_send()
 
     recv_all(msg_r, got_r, sr, rr, minus)
     returned = got_r[...].reshape(NC * SLOT, 128)
@@ -333,13 +349,8 @@
     near = gather_points(dot(own, expand[...]), P_FINE)
     near = [near[b] + near[3 + b] for b in range(3)]
     near = jnp.concatenate(near + [jnp.zeros((5, P_FINE), F32)], axis=0).astype(BF)
-    velocity = dot(near, sm[...])
-
-    z_next(3)
-    octant_rows = held[...].astype(F32).reshape(8 * NR, 128).astype(BF)
-    msg_f[...] = dot(counts[...], octant_rows).reshape(NC, 8, 128).astype(BF)
-    send_all(msg_f, got_f, sf, rf, minus)
-    got_f[0] = msg_f[0]
+    velocity = dot_nt(near, sm[...])
+
     recv_all(msg_f, got_f, sf, rf, minus)
     summed = jnp.sum(got_f[...].astype(F32), axis=0)
     turn = iota((8, 128), 0)
@@ -350,15 +361,10 @@
     far = [moved[:, 256 * b : 256 * b + EQ_PTS] for b in range(3)]
     far = jnp.concatenate(far + [jnp.zeros((5, EQ_PTS), F32)], axis=0).astype(BF)
     velocity = velocity + dot(far, smooth_hi[...]) + dot(far, smooth_lo[...])
-    out_ref[0] = velocity[0:3, :]
-
-    sent_all(msg_d, got_d, sd, rd, plus)
-    sent_all(msg_b, got_b, sb, rb, plus)
-    sent_all(msg_r, got_r, sr, rr, minus)
+    for comp in range(3):
+        out_ref[comp] = velocity[comp : comp + 1, :]
+
     sent_all(msg_f, got_f, sf, rf, minus)
-    for stage in stages:
-        for copy in stage:
-            copy.wait_send()
 
 
 def on_device(
@@ -367,21 +373,19 @@
 ):
     vmem = pl.BlockSpec(memory_space=pltpu.VMEM)
     anywhere = pl.BlockSpec(memory_space=pl.ANY)
-    owner_row = block_owner.reshape(1, NB)
-    octant = block_octant.reshape(1, NB)
     dma = pltpu.SemaphoreType.DMA
-    return pl.pallas_call(
+    made = pl.pallas_call(
         kernel,
-        out_shape=jax.ShapeDtypeStruct((1, 3, P_COARSE), F32),
-        in_specs=[vmem] * 5 + [anywhere] * 6,
+        out_shape=jax.ShapeDtypeStruct((3, 1, P_COARSE), F32),
+        in_specs=[vmem] * 4 + [anywhere] * 6,
         out_specs=vmem,
         scratch_shapes=[
             pltpu.VMEM((P_COARSE, P_FINE), BF),
             pltpu.VMEM((P_COARSE, P_FINE), BF),
-            pltpu.VMEM((P_FINE, EQ_PTS), BF),
+            pltpu.VMEM((EQ_PTS, P_FINE), BF),
             pltpu.VMEM((EQUIV, EQUIV), BF),
             pltpu.VMEM((EQ_PTS, P_FINE), BF),
-            pltpu.VMEM((P_FINE, P_COARSE), BF),
+            pltpu.VMEM((P_COARSE, P_FINE), BF),
             pltpu.VMEM((NB, P_FINE), BF),
             pltpu.VMEM((NC * SLOT, LEAF), BF),
             pltpu.VMEM((NC * SLOT, NB), BF),
@@ -412,8 +416,9 @@
         compiler_params=pltpu.CompilerParams(
             collective_id=0, has_side_effects=True, vmem_limit_bytes=60 * 1024 * 1024
         ),
-    )(cell_shape, owner_row, block_owner, octant, far_list,
-      upsample, bending, to_density, translate, evaluate, smoothing)
+    )(cell_shape, block_owner.reshape(1, NB), block_octant, far_list,
+      upsample, bending, to_density.T, translate, evaluate, smoothing.T)
+    return jnp.transpose(made, (1, 0, 2))
 
 
 def solution(mesh):

time: 72.6 us -> 59.8 us (0.82)
  local copies, waits for them, and re-layouts: 10.7 us -> 1.29 us
  Pallas kernels: 61.6 us -> 58.3 us
    unnamed x3 -> x1, local copies, waits for them, and re-layouts: 8.1 us -> 1.29 us
    pallas_call x1, Pallas kernels: 61.6 us -> 58.3 us  [on_device(): pl.pallas_call(kernel, out_shape=jax.ShapeDtypeStruct((3, 1, P_COARSE), F...]
    pallas_call x1 -> x0, local copies, waits for them, and re-layouts: 1.3 us -> none  [on_device(): pl.pallas_call(kernel, out_shape=jax.ShapeDtypeStruct((1, 3, P_COARSE), F...]
    reshape x1 -> x0, local copies, waits for them, and re-layouts: 1.24 us -> none  [on_device(): octant = block_octant.reshape(1, NB)]
where the time goes in v2:
time: 59.8 us; the launch traced here: 59.6 us
  Pallas kernels  58.3 us (97%)
  local copies, waits for them, and re-layouts  1.29 us (2%)
    pallas_call x1, Pallas kernels, on_device(): pl.pallas_call(kernel, out_shape=jax.ShapeDtypeStruct((3, 1, P_COARSE), F...  58.3 us
    unnamed x1, local copies, waits for them, and re-layouts  1.29 us

profile of v2, /device:TPU:1, one launch (start us, length us, event | category | flops | bytes accessed | tf_op | source)
XLA Modules:
  0.0 59.6 jit_solution(5432315789888246881)
XLA Ops:
  0.0 58.3 %shard_map.100 = f32[3,1,544]{2,1,0:T(1,128)} custom-call(bf16[1,3,544]{2,1,0:T(4,128)(2,1)} %cell_ref.1, s32[1,264]{1,0:T(1,128)} %bitcast.7, s32[264]{0:T(512)} %octant_ref.1, s32[1,8]{1,0:T(1,128)} %far_ref.1, bf16[544,2112]{1,0:T(8,128)(2,1)} %up_hbm.1, bf16[544,2112]{1,0:T(8,128)(2,1)} %bend_hbm.1, bf16[152,2112]{1,0:T(8,128)(2,1)} %bitcast.5, ...), custom_call_target="tpu_custom_call" | custom-call | tf_op jit(solution)/shard_map/pallas_call | solution.py:377
  58.3 1.3 %copy.12 = f32[1,3,544]{2,0,1:T(1,128)} copy(f32[1,3,544]{2,0,1:T(1,128)} %bitcast.6) | data formatting | bytes 13056
